TPU v7x, 256 devices: a whole 4x4x8 slice. The times are simulated.
256 devices in a mesh: pair: 64 (over y, z, core), virt: 4 (over x).
Axes of the slice: x: 4, y: 4, z: 8, core: 2. Of those that a mesh axis runs over, the one named last changes fastest.
Arguments:
- amplitudes: bfloat16 [2048, 128, 1024], P('pair', 'virt'), may hold values from -6 to 6
- amp_pairs: int32 [2048], P('pair'), may hold values from 0 to 16383, as said below
- pair_map: int32 [16384], replicated, may hold values from -1 to 511, as said below
- integrals: bfloat16 [512, 2, 1024, 1024], P('pair', None, None, 'virt'), may hold values from -0.1875 to 0.1875
- block_cols: int32 [512, 2], P('pair'), may hold values from 0 to 16383, as said below
- occ_energy: float32 [8192], P('pair'), may hold values from -3 to -0.7
- virt_energy: float32 [4096], replicated, may hold values from 0.3 to 2
Outputs:
- update: bfloat16 [2048, 128, 1024], P('pair', None, 'virt')
Inputs may be any that keep to these rules, and one draw needn't show every extreme that they name: `amp_pairs`: within one occupied tile (tiles k * 32 to k * 32 + 31) the pairs differ and each has a row in pair_map. Consecutive occupied tiles form groups that hold the same set of pairs, and a pair belongs to one group only. `pair_map`: exactly 512 entries are not -1: the rows 0 to 511, once each, at the pairs that occur in amp_pairs. Row u lies on pair index u // 8. The pairs of one occupied tile have at most 1 row on any one pair index, and some reach 1. At most 8 occupied tiles hold the pair of any one row, and some row is held by exactly 8. `block_cols`: the 2 entries of a row differ, and each is a pair of the group of occupied tiles that holds the row's own pair.
All inputs are finite; a program needn't handle non-finite values.
Results may differ from a plain program's by a relative error of at most 0.0049.
Values may be sent and summed in bfloat16 or wider, within the bound.
A program may use at most 128 MiB of HBM per device.

v0:
```python
import jax
import jax.numpy as jnp
from jax import lax
from jax.sharding import PartitionSpec as P

VTILE = 32


def local(amplitudes, amp_pairs, pair_map, integrals, block_cols, occ_energy, virt_energy):
    tile_count = amplitudes.shape[0]
    pair_devices = lax.axis_size("pair")
    virt_devices = lax.axis_size("virt")
    capacity = -(-tile_count // pair_devices)
    row_limit = min(8, pair_devices - pair_devices // 4 + 1)
    local_rows = integrals.shape[0]
    block_count = integrals.shape[1]
    full_width = integrals.shape[2]
    part_width = integrals.shape[3]
    occ_rows = occ_energy.shape[0]
    send_slots = pair_devices * capacity
    row_of_tile = pair_map[amp_pairs]
    present = row_of_tile >= 0
    owner_pair = row_of_tile // local_rows
    order_index = jnp.arange(tile_count, dtype=jnp.int32)
    earlier = (
        (owner_pair[:, None] == owner_pair[None, :])
        & (order_index[None, :] < order_index[:, None])
        & present[None, :]
    )
    slot_rank = jnp.sum(earlier.astype(jnp.int32), axis=1)
    destination = jnp.where(present, owner_pair * capacity + slot_rank, send_slots)
    target_rows = (
        jnp.full((send_slots,), -1, jnp.int32)
        .at[destination]
        .set(row_of_tile % local_rows, mode="drop")
    )
    sender_pairs = jnp.broadcast_to(amp_pairs[None, None, :], (pair_devices, capacity, tile_count))
    local_row_ids = jnp.arange(local_rows, dtype=jnp.int32)
    outgoing = lax.all_gather(amplitudes, "virt", axis=1, tiled=True)
    send_tiles = (
        jnp.zeros((send_slots,) + outgoing.shape[1:], jnp.bfloat16)
        .at[destination]
        .set(outgoing, mode="drop")
    )
    packed = (
        send_tiles.reshape((pair_devices, capacity) + outgoing.shape[1:]),
        target_rows.reshape(pair_devices, capacity),
        sender_pairs,
    )
    arrived = lax.all_to_all(packed[0], "pair", split_axis=0, concat_axis=0, tiled=True)
    arrived_rows = lax.all_to_all(packed[1], "pair", split_axis=0, concat_axis=0, tiled=True)
    arrived_pairs = lax.all_to_all(packed[2], "pair", split_axis=0, concat_axis=0, tiled=True)
    sources = arrived.shape[0]
    item_count = arrived.shape[1]
    slot_total = sources * item_count
    tile_height = arrived.shape[2]
    flat_tiles = arrived.reshape(slot_total, tile_height, full_width)
    flat_rows = arrived_rows.reshape(slot_total)
    flat_pairs = arrived_pairs.reshape(slot_total, tile_count)
    slot_index = jnp.arange(slot_total, dtype=jnp.int32)
    limit_index = jnp.arange(row_limit, dtype=jnp.int32)

    def row_step(row_index, products):
        hit_mask = flat_rows == row_index
        hit_rank = jnp.cumsum(hit_mask.astype(jnp.int32)) - 1
        picked = hit_mask[None, :] & (hit_rank[None, :] == limit_index[:, None])
        occupied = jnp.any(picked, axis=1)
        chosen_slot = jnp.sum(picked.astype(jnp.int32) * slot_index[None, :], axis=1)
        gathered = flat_tiles[chosen_slot].reshape(row_limit * tile_height, full_width)
        row_blocks = lax.dynamic_index_in_dim(integrals, row_index, 0, keepdims=False)
        result = jnp.einsum("kd,mdc->kmc", gathered, row_blocks, preferred_element_type=jnp.float32)
        result = result.astype(jnp.bfloat16).reshape(
            row_limit, tile_height, block_count, part_width
        )
        return products.at[jnp.where(occupied, chosen_slot, slot_total)].set(result, mode="drop")

    empty_products = jnp.zeros((slot_total, tile_height, block_count, part_width), jnp.bfloat16)
    products = lax.fori_loop(0, local_rows, row_step, empty_products)
    row_hot = (flat_rows[:, None] == local_row_ids[None, :]).astype(jnp.int32)
    column_pair = jnp.sum(row_hot[:, :, None] * block_cols[None, :, :], axis=1)
    landing = flat_pairs[:, None, :] == column_pair[:, :, None]
    matched = jnp.any(landing, axis=2) & (flat_rows >= 0)[:, None]
    target = jnp.where(
        matched, jnp.sum(landing.astype(jnp.int32) * order_index[None, None, :], axis=2), tile_count
    )
    returned_back = (
        lax.all_to_all(
            products.reshape(sources, item_count, tile_height, block_count, part_width),
            "pair",
            split_axis=0,
            concat_axis=0,
            tiled=True,
        ),
        lax.all_to_all(
            target.reshape(sources, item_count, block_count),
            "pair",
            split_axis=0,
            concat_axis=0,
            tiled=True,
        ),
    )
    back_tiles, back_targets = returned_back
    landing_hot = (back_targets[None] == order_index[:, None, None, None]).astype(jnp.bfloat16)
    ladder = jnp.einsum(
        "apqm,pqimc->aic", landing_hot, back_tiles, preferred_element_type=jnp.float32
    )
    virt_tiles = virt_energy.shape[0] // VTILE
    energy_table = virt_energy.reshape(virt_tiles, VTILE)
    tile_ids = jnp.arange(virt_tiles, dtype=jnp.int32)
    onehot_first = (amp_pairs[:, None] // virt_tiles == tile_ids[None, :]).astype(jnp.float32)
    onehot_second = (amp_pairs[:, None] % virt_tiles == tile_ids[None, :]).astype(jnp.float32)
    energy_first = jnp.dot(onehot_first, energy_table, precision=lax.Precision.HIGHEST)
    energy_second = jnp.dot(onehot_second, energy_table, precision=lax.Precision.HIGHEST)
    per_device = VTILE // virt_devices
    energy_first = lax.dynamic_slice_in_dim(
        energy_first, lax.axis_index("virt") * per_device, per_device, 1
    )
    denominator = (
        energy_first[:, None, :, None]
        + energy_second[:, None, None, :]
        - occ_energy[None, :, None, None]
    )
    denominator = denominator.reshape(tile_count, occ_rows, part_width)
    return (ladder / denominator).astype(jnp.bfloat16)


def solution(mesh):
    in_specs = (
        P("pair", "virt", None),
        P("pair"),
        P(),
        P("pair", None, None, "virt"),
        P("pair", None),
        P("pair"),
        P(),
    )
    out_specs = P("pair", None, "virt")
    return jax.shard_map(local, mesh=mesh, in_specs=in_specs, out_specs=out_specs, check_vma=False)
```

profile of v0, /device:TPU:1, one launch (start us, length us, event | category | flops | bytes accessed | tf_op | source)
XLA Modules:
  0.0 846.5 jit_solution(6966731193070125893)
XLA Ops:
  6.5 0.7 all-gather.2.cloned.1.call-update
  7.3 0.7 and_select_fusion.1
  7.9 0.7 gather_fusion.1
  8.7 0.2 convert_reduce_fusion
  8.9 0.7 scatter_custom_fusion.1
  9.6 22.2 %all_to_all.29 = s32[64,1,1]{2,1,0:T(1,128)S(1)} all-to-all(s32[64,1,1]{2,1,0:T(1,128)S(1)} %copy.52), channel_id=1, replica_groups=mesh['pair'=64,'virt'=4] {'pair'}, dimensions={0} | all-to-all | bytes 512 | tf_op jit(solution)/shard_map/all_to_all | solution.py:51
  31.9 1.3 broadcast_in_dim.42
  33.2 4.7 all-to-all-start
  37.9 60.8 %all-gather.2.cloned.1.call-done = bf16[32,128,1024]{2,1,0:T(8,128)(2,1)} async-done(((bf16[32,32,1024]{2,1,0:T(8,128)(2,1)}), bf16[32,128,1024]{2,1,0:T(8,128)(2,1)}) %all-gather.2.cloned.1.call-update) | async-done | bytes 8388624 | tf_op jit(solution)/shard_map/all_gather | solution.py:39
  98.6 6.0 broadcast_in_dim.78
  104.6 21.4 %scatter_fusion.1 = bf16[64,128,1024]{2,1,0:T(8,128)(2,1)} fusion(bf16[64,128,1024]{2,1,0:T(8,128)(2,1)} %broadcast_in_dim.78, s32[32]{0:T(128)S(1)} %fusion.30, bf16[32,128,1024]{2,1,0:T(8,128)(2,1)} %all-gather.2.cloned.1.call-done), kind=kCustom, calls=%fused_computation.4 | custom fusion | bytes 25165952 | tf_op jit(solution)/shard_map/scatter | solution.py:43
  126.0 11.2 %all-to-all-start.3 = ((bf16[64,1,128,1024]{3,2,1,0:T(8,128)(2,1)}), bf16[64,1,128,1024]{3,2,1,0:T(8,128)(2,1)}, u32[]{:S(2)}, u32[]{:S(2)}) async-start(bf16[64,1,128,1024]{3,2,1,0:T(8,128)(2,1)} %bitcast.89), calls=%async_computation.3 | async-start | bytes 33554432 | tf_op jit(solution)/shard_map/all_to_all | solution.py:50
  137.2 1.2 reduce.1
  138.7 0.7 copy.53
  139.4 363.4 %all-to-all-done.3 = bf16[64,1,128,1024]{3,2,1,0:T(8,128)(2,1)} async-done(((bf16[64,1,128,1024]{3,2,1,0:T(8,128)(2,1)}), bf16[64,1,128,1024]{3,2,1,0:T(8,128)(2,1)}, u32[]{:S(2)}, u32[]{:S(2)}) %all-to-all-start.3) | async-done | bytes 16777248 | tf_op jit(solution)/shard_map/all_to_all | solution.py:50
  502.7 6.1 all-to-all-start.2
  508.8 4.3 broadcast_in_dim.47
  513.1 98.7 %while.16 = (s32[]{:T(128)}, bf16[64,128,2,256]{3,1,2,0:T(8,128)(2,1)}, s32[64]{0:T(128)S(1)}, bf16[64,128,1024]{2,1,0:T(8,128)(2,1)}, bf16[8,2,1024,256]{3,2,1,0:T(8,128)(2,1)}, /*index=5*/s32[]{:T(128)}, s32[]{:T(128)}) while((s32[]{:T(128)}, bf16[64,128,2,256]{3,1,2,0:T(8,128)(2,1)}, s32[64]{0:T(128)S(1)}, ...), condition=%wide.region_11.12_spmd.clone, body=%wide.region_6.11_spmd.clone.sunk | while | flops 1074274944 | bytes 13639173 | solution.py:78
  513.4 0.1 fusion.44
  513.5 0.1 fusion.43
  513.7 6.5 gather_fusion
  520.1 2.5 convolution_convert_fusion.2
  522.7 2.8 scatter_fusion
  525.8 0.1 fusion.44
  525.9 0.1 fusion.43
  526.1 6.5 gather_fusion
  532.5 2.5 convolution_convert_fusion.2
  535.1 2.7 scatter_fusion
  538.1 0.1 fusion.44
  538.4 6.5 gather_fusion
  544.8 2.5 convolution_convert_fusion.2
  547.4 2.7 scatter_fusion
  550.4 0.1 fusion.44
  550.5 0.1 fusion.43
  550.7 6.5 gather_fusion
  557.1 2.5 convolution_convert_fusion.2
  559.7 2.8 scatter_fusion
  562.8 0.1 fusion.44
  562.9 0.1 fusion.43
  563.1 6.5 gather_fusion
  569.5 2.5 convolution_convert_fusion.2
  572.1 2.7 scatter_fusion
  575.1 0.1 fusion.44
  575.2 0.1 fusion.43
  575.3 6.5 gather_fusion
  581.8 2.5 convolution_convert_fusion.2
  584.4 2.7 scatter_fusion
  587.4 0.1 fusion.44
  587.7 6.5 gather_fusion
  594.1 2.5 convolution_convert_fusion.2
  596.7 2.8 scatter_fusion
  599.7 0.1 fusion.44
  599.9 0.1 fusion.43
  600.0 6.5 gather_fusion
  606.5 2.5 convolution_convert_fusion.2
  609.0 2.7 scatter_fusion
  611.7 16.3 %copy.67 = bf16[64,128,2,256]{3,2,1,0:T(2,128)(2,1)} copy(bf16[64,128,2,256]{3,1,2,0:T(8,128)(2,1)} %get-tuple-element.181) | data formatting | bytes 16777216 | tf_op jit(solution)/shard_map/while | solution.py:78
  628.0 10.5 %all-to-all-start.4 = ((bf16[64,1,128,2,256]{4,3,2,1,0:T(2,128)(2,1)}), bf16[64,1,128,2,256]{4,3,2,1,0:T(2,128)(2,1)}, u32[]{:S(2)}, u32[]{:S(2)}) async-start(bf16[64,1,128,2,256]{4,3,2,1,0:T(2,128)(2,1)} %bitcast.91), calls=%async_computation.4 | async-start | bytes 16777216 | tf_op jit(solution)/shard_map/all_to_all | solution.py:87
  638.6 0.2 fusion.24
  638.9 0.2 fusion.25
  639.1 0.1 broadcast_add_fusion
  639.4 184.9 %all-to-all-done.4 = bf16[64,1,128,2,256]{4,3,2,1,0:T(2,128)(2,1)} async-done(((bf16[64,1,128,2,256]{4,3,2,1,0:T(2,128)(2,1)}), bf16[64,1,128,2,256]{4,3,2,1,0:T(2,128)(2,1)}, u32[]{:S(2)}, u32[]{:S(2)}) %all-to-all-start.4) | async-done | bytes 8388640 | tf_op jit(solution)/shard_map/all_to_all | solution.py:87
  824.3 12.9 %fusion.15 = bf16[32,128,256]{2,0,1:T(8,128)(2,1)S(1)} fusion(bf16[64,1,128,2,256]{4,3,2,1,0:T(2,128)(2,1)} %all-to-all-done.4, f32[128]{0:T(128)S(1)} %copy-done.4, f32[32,256]{1,0:T(8,128)S(1)} %add.165, s32[64,2]{0,1:T(2,128)S(1)} %bitcast.94), kind=kOutput, calls=%fused_computation.30 | convolution fusion | flops 271585280 | bytes 10519552 | tf_op jit(solution)/shard_map/apqm,pqimc->aic/dot_general | solution.py:104
  837.2 2.5 copy.58
  (88 shorter events, 4.0 us)
Async XLA Ops:
  6.5 1.4 copy-start
  6.5 92.1 %all-gather.2.cloned.1.call-start = ((), (), s32[]{:S(2)}) async-start(), calls=%async_computation.5 | async-start | bytes 10485760 | tf_op jit(solution)/shard_map/all_gather | solution.py:39
  33.2 92.8 %all-to-all-start = ((s32[64,1,32]{2,1,0:T(1,128)}), s32[64,1,32]{2,1,0:T(1,128)S(1)}, u32[]{:S(2)}, u32[]{:S(2)}) async-start(s32[64,1,32]{2,1,0:T(1,128)} %broadcast_in_dim.42), calls=%async_computation | async-start | bytes 65536 | tf_op jit(solution)/shard_map/all_to_all | solution.py:52
  126.0 12.4 %copy-start.3 = (s32[8,2]{0,1:T(2,128)S(1)}, s32[8,2]{0,1:T(2,128)}, u32[]{:S(2)}) copy-start(s32[8,2]{0,1:T(2,128)} %param.13) | copy-start | bytes 196
  126.0 376.7 %all-to-all-start.3 = ((bf16[64,1,128,1024]{3,2,1,0:T(8,128)(2,1)}), bf16[64,1,128,1024]{3,2,1,0:T(8,128)(2,1)}, u32[]{:S(2)}, u32[]{:S(2)}) async-start(bf16[64,1,128,1024]{3,2,1,0:T(8,128)(2,1)} %bitcast.89), calls=%async_computation.3 | async-start | bytes 33554432 | tf_op jit(solution)/shard_map/all_to_all | solution.py:50
  502.7 125.3 %all-to-all-start.2 = ((s32[64,1,2]{2,1,0:T(1,128)}), s32[64,1,2]{2,1,0:T(1,128)S(1)}, u32[]{:S(2)}, u32[]{:S(2)}) async-start(s32[64,1,2]{2,1,0:T(1,128)} %copy.53), calls=%async_computation.2 | async-start | bytes 65536 | tf_op jit(solution)/shard_map/all_to_all | solution.py:94
  628.0 10.5 %copy-start.2 = (f32[4096]{0:T(1024)S(1)}, f32[4096]{0:T(1024)}, u32[]{:S(2)}) copy-start(f32[4096]{0:T(1024)} %param.15) | copy-start | bytes 49156
  628.0 196.3 %copy-start.4 = (f32[128]{0:T(128)S(1)}, f32[128]{0:T(128)}, u32[]{:S(2)}) copy-start(f32[128]{0:T(128)} %param.14) | copy-start | bytes 1540
  628.0 196.2 %all-to-all-start.4 = ((bf16[64,1,128,2,256]{4,3,2,1,0:T(2,128)(2,1)}), bf16[64,1,128,2,256]{4,3,2,1,0:T(2,128)(2,1)}, u32[]{:S(2)}, u32[]{:S(2)}) async-start(bf16[64,1,128,2,256]{4,3,2,1,0:T(2,128)(2,1)} %bitcast.91), calls=%async_computation.4 | async-start | bytes 16777216 | tf_op jit(solution)/shard_map/all_to_all | solution.py:87
  824.3 15.4 %copy-start.1 = (s32[16384]{0:T(1024)S(1)}, s32[16384]{0:T(1024)}, u32[]{:S(2)}) copy-start(s32[16384]{0:T(1024)} %param.11) | copy-start | bytes 196612
Sparse Core Ops, SparseCore 0:
  9.2 89.4 all-gather.1
where the time goes:
time: 848 us; the launch traced here: 847 us
  waiting for transfers between devices  610 us (72%)
  local copies, waits for them, and re-layouts  129 us (15%)
  matrix products  33.1 us (4%)
  starting transfers between devices  32.4 us (4%)
  blocking collectives  22.2 us (3%)
  between operations  13.5 us (2%)
    all_to_all x1, waiting for transfers between devices, local(): lax.all_to_all(packed[0], 'pair', split_axis=0, concat_axis=0, tiled=True)  363 us
    all_to_all x1, waiting for transfers between devices, local(): lax.all_to_all(products.reshape(sources, item_count, tile_height, block_c...  185 us
    all_gather x1, waiting for transfers between devices, local(): outgoing = lax.all_gather(amplitudes, 'virt', axis=1, tiled=True)  60.8 us
    gather x8, local copies, waits for them, and re-layouts, row_step(): flat_tiles[chosen_slot].reshape(row_limit * tile_height, full_width)  51.6 us
    all_to_all x1, blocking collectives, local(): lax.all_to_all(packed[1], 'pair', split_axis=0, concat_axis=0, tiled=True)  22.2 us
    scatter x8, local copies, waits for them, and re-layouts, row_step(): products.at[jnp.where(occupied, chosen_slot, slot_total)]  21.9 us
    scatter x1, local copies, waits for them, and re-layouts, local(): send_tiles = jnp.zeros((send_slots,) + outgoing.shape[1:], jnp.bfloat16)....  21.4 us
    dot_general x8, matrix products, row_step(): jnp.einsum('kd,mdc->kmc', gathered, row_blocks, preferred_element_type=jn...  19.8 us
  transfers between devices with their start and end apart: 5, of which 3 were waited for; matrix products, arithmetic and copies ran while one was open for 18% of the time, Pallas kernels for 0%

commit v1 on v0

--- a/solution.py
+++ b/solution.py
@@ -4,6 +4,16 @@
 from jax.sharding import PartitionSpec as P
 
 VTILE = 32
+
+
+def gather_by_hops(shard, axis, d):
+    size = lax.axis_size(axis)
+    block, blocks = (shard, [shard])
+    for _ in range(size - 1):
+        block = lax.ppermute(block, axis, [(i, (i + 1) % size) for i in range(size)])
+        blocks.insert(0, block)
+    line = jnp.concatenate(blocks, axis=d)
+    return jnp.roll(line, (lax.axis_index(axis) + 1) * shard.shape[d], axis=d)
 
 
 def local(amplitudes, amp_pairs, pair_map, integrals, block_cols, occ_energy, virt_energy):
@@ -36,7 +46,7 @@
     )
     sender_pairs = jnp.broadcast_to(amp_pairs[None, None, :], (pair_devices, capacity, tile_count))
     local_row_ids = jnp.arange(local_rows, dtype=jnp.int32)
-    outgoing = lax.all_gather(amplitudes, "virt", axis=1, tiled=True)
+    outgoing = gather_by_hops(amplitudes, "virt", 1)
     send_tiles = (
         jnp.zeros((send_slots,) + outgoing.shape[1:], jnp.bfloat16)
         .at[destination]

time: 848 us -> 928 us (1.094)
  waiting for transfers between devices: 610 us -> 663 us
  starting transfers between devices: 32.4 us -> 66.8 us
  local copies, waits for them, and re-layouts: 129 us -> 157 us
  blocking collectives: 22.2 us -> 0 us
  between operations: 13.5 us -> 0.19 us
    ppermute x0 -> x3, waiting for transfers between devices: none -> 114 us  [gather_by_hops(): lax.ppermute(block, axis, [(i, (i + 1) % size) for i in range(size)])]
    all_gather x1 -> x0, waiting for transfers between devices: 60.8 us -> none  [local(): outgoing = lax.all_gather(amplitudes, 'virt', axis=1, tiled=True)]
    all_to_all x1 -> x0, blocking collectives: 22.2 us -> none  [local(): lax.all_to_all(packed[1], 'pair', split_axis=0, concat_axis=0, tiled=True)]
    unnamed x10 -> x25, local copies, waits for them, and re-layouts: 0.02 us -> 18.3 us
    all_to_all x0 -> x1, starting transfers between devices: none -> 16 us  [local(): lax.all_to_all(packed[1], 'pair', split_axis=0, concat_axis=0, tiled=True)]
    all_to_all x1, starting transfers between devices: 4.69 us -> 18.9 us  [local(): lax.all_to_all(packed[2], 'pair', split_axis=0, concat_axis=0, tiled=True)]
  transfers between devices with their start and end apart: 5 -> 8, of which waited for: 3 -> 5; matrix products, arithmetic and copies ran while one was open for 18% -> 19% of each run, Pallas kernels for 0% -> 0%
where the time goes in v1:
time: 928 us; the launch traced here: 926 us
  waiting for transfers between devices  663 us (71%)
  local copies, waits for them, and re-layouts  157 us (17%)
  starting transfers between devices  66.8 us (7%)
  matrix products  33.1 us (4%)
    all_to_all x1, waiting for transfers between devices, local(): lax.all_to_all(packed[0], 'pair', split_axis=0, concat_axis=0, tiled=True)  363 us
    all_to_all x1, waiting for transfers between devices, local(): lax.all_to_all(products.reshape(sources, item_count, tile_height, block_c...  185 us
    ppermute x3, waiting for transfers between devices, gather_by_hops(): lax.ppermute(block, axis, [(i, (i + 1) % size) for i in range(size)])  114 us
    gather x8, local copies, waits for them, and re-layouts, row_step(): flat_tiles[chosen_slot].reshape(row_limit * tile_height, full_width)  51.6 us
    scatter x8, local copies, waits for them, and re-layouts, row_step(): products.at[jnp.where(occupied, chosen_slot, slot_total)]  21.9 us
    scatter x1, local copies, waits for them, and re-layouts, local(): send_tiles = jnp.zeros((send_slots,) + outgoing.shape[1:], jnp.bfloat16)....  21.4 us
    dot_general x8, matrix products, row_step(): jnp.einsum('kd,mdc->kmc', gathered, row_blocks, preferred_element_type=jn...  19.8 us
    all_to_all x1, starting transfers between devices, local(): lax.all_to_all(packed[2], 'pair', split_axis=0, concat_axis=0, tiled=True)  18.9 us
  transfers between devices with their start and end apart: 8, of which 5 were waited for; matrix products, arithmetic and copies ran while one was open for 19% of the time, Pallas kernels for 0%

profile of v1, /device:TPU:1, one launch (start us, length us, event | category | flops | bytes accessed | tf_op | source)
XLA Modules:
  0.0 926.1 jit_solution(9679516669906909615)
XLA Ops:
  0.0 2.0 collective-permute-start
  2.0 44.6 %collective-permute-done = bf16[32,32,1024]{2,1,0:T(8,128)(2,1)S(1)} collective-permute-done((bf16[32,32,1024]{2,1,0:T(8,128)(2,1)}, bf16[32,32,1024]{2,1,0:T(8,128)(2,1)S(1)}, u32[]{:S(2)}, u32[]{:S(2)}) %collective-permute-start) | collective-permute-done | bytes 2097184 | tf_op jit(solution)/shard_map/ppermute | solution.py:13
  46.6 1.3 copy-done.3
  48.0 1.8 collective-permute-start.1
  49.8 44.6 %collective-permute-done.1 = bf16[32,32,1024]{2,1,0:T(8,128)(2,1)} collective-permute-done((bf16[32,32,1024]{2,1,0:T(8,128)(2,1)S(1)}, bf16[32,32,1024]{2,1,0:T(8,128)(2,1)}, u32[]{:S(2)}, u32[]{:S(2)}) %collective-permute-start.1) | collective-permute-done | bytes 2097184 | tf_op jit(solution)/shard_map/ppermute | solution.py:13
  94.3 0.8 collective-permute-start.2
  95.1 0.7 and_select_fusion.1
  95.8 0.7 gather_fusion.1
  96.5 0.2 convert_reduce_fusion
  96.7 0.7 scatter_custom_fusion.1
  97.4 0.7 copy.52
  98.1 16.0 %all-to-all-start.1 = ((s32[64,1,1]{2,1,0:T(1,128)}), s32[64,1,1]{2,1,0:T(1,128)S(1)}, u32[]{:S(2)}, u32[]{:S(2)}) async-start(s32[64,1,1]{2,1,0:T(1,128)} %copy.52), calls=%async_computation.1 | async-start | bytes 65536 | tf_op jit(solution)/shard_map/all_to_all | solution.py:61
  114.1 25.2 %collective-permute-done.2 = bf16[32,32,1024]{2,1,0:T(8,128)(2,1)} collective-permute-done((bf16[32,32,1024]{2,1,0:T(8,128)(2,1)}, bf16[32,32,1024]{2,1,0:T(8,128)(2,1)}, u32[]{:S(2)}, u32[]{:S(2)}) %collective-permute-start.2) | collective-permute-done | bytes 2097184 | tf_op jit(solution)/shard_map/ppermute | solution.py:13
  139.3 3.1 constant_dynamic-update-slice_fusion.7
  142.5 3.1 constant_dynamic-update-slice_fusion.6
  145.6 1.4 constant_dynamic-update-slice_fusion.5
  147.0 1.5 constant_dynamic-update-slice_fusion.4
  148.5 3.2 constant_dynamic-update-slice_fusion.3
  151.7 3.1 constant_dynamic-update-slice_fusion.2
  154.8 1.4 constant_dynamic-update-slice_fusion.1
  156.3 1.5 constant_dynamic-update-slice_fusion
  157.8 0.6 broadcast_in_dim.42
  158.4 18.9 %all-to-all-start = ((s32[64,1,32]{2,1,0:T(1,128)}), s32[64,1,32]{2,1,0:T(1,128)S(1)}, u32[]{:S(2)}, u32[]{:S(2)}) async-start(s32[64,1,32]{2,1,0:T(1,128)} %broadcast_in_dim.42), calls=%async_computation | async-start | bytes 65536 | tf_op jit(solution)/shard_map/all_to_all | solution.py:62
  177.3 8.2 constant_dynamic-slice_fusion.1
  185.5 6.0 broadcast_in_dim.78
  191.5 21.4 %scatter_fusion.1 = bf16[64,128,1024]{2,1,0:T(8,128)(2,1)} fusion(bf16[64,128,1024]{2,1,0:T(8,128)(2,1)} %broadcast_in_dim.78, s32[32]{0:T(128)S(1)} %fusion.30, bf16[32,128,1024]{2,1,0:T(8,128)(2,1)} %constant_dynamic-slice_fusion.1), kind=kCustom, calls=%fused_computation.4 | custom fusion | bytes 25165952 | tf_op jit(solution)/shard_map/scatter | solution.py:53
  212.9 10.8 %all-to-all-start.3 = ((bf16[64,1,128,1024]{3,2,1,0:T(8,128)(2,1)}), bf16[64,1,128,1024]{3,2,1,0:T(8,128)(2,1)}, u32[]{:S(2)}, u32[]{:S(2)}) async-start(bf16[64,1,128,1024]{3,2,1,0:T(8,128)(2,1)} %bitcast.89), calls=%async_computation.3 | async-start | bytes 33554432 | tf_op jit(solution)/shard_map/all_to_all | solution.py:60
  223.7 1.2 reduce.1
  225.1 0.7 copy.53
  225.8 363.4 %all-to-all-done.3 = bf16[64,1,128,1024]{3,2,1,0:T(8,128)(2,1)} async-done(((bf16[64,1,128,1024]{3,2,1,0:T(8,128)(2,1)}), bf16[64,1,128,1024]{3,2,1,0:T(8,128)(2,1)}, u32[]{:S(2)}, u32[]{:S(2)}) %all-to-all-start.3) | async-done | bytes 16777248 | tf_op jit(solution)/shard_map/all_to_all | solution.py:60
  589.2 6.1 all-to-all-start.2
  595.3 4.3 broadcast_in_dim.47
  599.6 98.7 %while.16 = (s32[]{:T(128)}, bf16[64,128,2,256]{3,1,2,0:T(8,128)(2,1)}, s32[64]{0:T(128)S(1)}, bf16[64,128,1024]{2,1,0:T(8,128)(2,1)}, bf16[8,2,1024,256]{3,2,1,0:T(8,128)(2,1)}, /*index=5*/s32[]{:T(128)}, s32[]{:T(128)}) while((s32[]{:T(128)}, bf16[64,128,2,256]{3,1,2,0:T(8,128)(2,1)}, s32[64]{0:T(128)S(1)}, ...), condition=%wide.region_11.12_spmd.clone, body=%wide.region_6.11_spmd.clone.sunk | while | flops 1074274944 | bytes 13639173 | solution.py:88
  600.1 6.5 gather_fusion
  606.6 2.5 convolution_convert_fusion.2
  609.2 2.8 scatter_fusion
  612.5 6.5 gather_fusion
  619.0 2.5 convolution_convert_fusion.2
  621.5 2.7 scatter_fusion
  624.8 6.5 gather_fusion
  631.3 2.5 convolution_convert_fusion.2
  633.9 2.7 scatter_fusion
  637.1 6.5 gather_fusion
  643.6 2.5 convolution_convert_fusion.2
  646.2 2.8 scatter_fusion
  649.5 6.5 gather_fusion
  656.0 2.5 convolution_convert_fusion.2
  658.5 2.7 scatter_fusion
  661.8 6.5 gather_fusion
  668.3 2.5 convolution_convert_fusion.2
  670.8 2.7 scatter_fusion
  674.1 6.5 gather_fusion
  680.6 2.5 convolution_convert_fusion.2
  683.1 2.8 scatter_fusion
  686.5 6.5 gather_fusion
  692.9 2.5 convolution_convert_fusion.2
  695.5 2.7 scatter_fusion
  698.2 16.3 %copy.67 = bf16[64,128,2,256]{3,2,1,0:T(2,128)(2,1)} copy(bf16[64,128,2,256]{3,1,2,0:T(8,128)(2,1)} %get-tuple-element.181) | data formatting | bytes 16777216 | tf_op jit(solution)/shard_map/while | solution.py:88
  714.5 10.5 %all-to-all-start.4 = ((bf16[64,1,128,2,256]{4,3,2,1,0:T(2,128)(2,1)}), bf16[64,1,128,2,256]{4,3,2,1,0:T(2,128)(2,1)}, u32[]{:S(2)}, u32[]{:S(2)}) async-start(bf16[64,1,128,2,256]{4,3,2,1,0:T(2,128)(2,1)} %bitcast.91), calls=%async_computation.4 | async-start | bytes 16777216 | tf_op jit(solution)/shard_map/all_to_all | solution.py:97
  725.0 0.2 fusion.24
  725.4 0.2 fusion.25
  725.9 184.9 %all-to-all-done.4 = bf16[64,1,128,2,256]{4,3,2,1,0:T(2,128)(2,1)} async-done(((bf16[64,1,128,2,256]{4,3,2,1,0:T(2,128)(2,1)}), bf16[64,1,128,2,256]{4,3,2,1,0:T(2,128)(2,1)}, u32[]{:S(2)}, u32[]{:S(2)}) %all-to-all-start.4) | async-done | bytes 8388640 | tf_op jit(solution)/shard_map/all_to_all | solution.py:97
  910.7 12.9 %fusion.15 = bf16[32,128,256]{2,0,1:T(8,128)(2,1)S(1)} fusion(bf16[64,1,128,2,256]{4,3,2,1,0:T(2,128)(2,1)} %all-to-all-done.4, f32[128]{0:T(128)S(1)} %copy-done.8, f32[32,256]{1,0:T(8,128)S(1)} %add.181, s32[64,2]{0,1:T(2,128)S(1)} %bitcast.94), kind=kOutput, calls=%fused_computation.30 | convolution fusion | flops 271585280 | bytes 10519552 | tf_op jit(solution)/shard_map/apqm,pqimc->aic/dot_general | solution.py:114
  923.6 2.5 copy.58
  (109 shorter events, 5.7 us)
Async XLA Ops:
  0.0 95.8 %copy-start = (s32[16384]{0:T(1024)S(1)}, s32[16384]{0:T(1024)}, u32[]{:S(2)}) copy-start(s32[16384]{0:T(1024)} %param.11) | copy-start | bytes 196612
  0.0 147.0 %copy-start.2 = (bf16[32,32,1024]{2,1,0:T(8,128)(2,1)S(1)}, bf16[32,32,1024]{2,1,0:T(8,128)(2,1)}, u32[]{:S(2)}) copy-start(bf16[32,32,1024]{2,1,0:T(8,128)(2,1)} %param.9) | copy-start | bytes 6291460
  0.0 46.6 %collective-permute-start = (bf16[32,32,1024]{2,1,0:T(8,128)(2,1)}, bf16[32,32,1024]{2,1,0:T(8,128)(2,1)S(1)}, u32[]{:S(2)}, u32[]{:S(2)}) collective-permute-start(bf16[32,32,1024]{2,1,0:T(8,128)(2,1)} %param.9), channel_id=1, source_target_pairs={{0,1},{1,2},{2,3},{3,0},{4,5},{5,6},{6,7},{7,4},{8,9},{9,10},{10,1... | collective-permute-start | bytes 6291464 | tf_op jit(solution)/shard_map/ppermute | solution.py:13
  46.6 1.3 copy-start.3
  48.0 46.4 %collective-permute-start.1 = (bf16[32,32,1024]{2,1,0:T(8,128)(2,1)S(1)}, bf16[32,32,1024]{2,1,0:T(8,128)(2,1)}, u32[]{:S(2)}, u32[]{:S(2)}) collective-permute-start(bf16[32,32,1024]{2,1,0:T(8,128)(2,1)S(1)} %collective-permute-done), channel_id=1, source_target_pairs={{0,1},{1,2},{2,3},{3,0},{4,5},{5,6},{6,7},{7,4},{8,9},{9,10},{10,1... | collective-permute-start | bytes 6291464 | tf_op jit(solution)/shard_map/ppermute | solution.py:13
  94.3 45.0 %collective-permute-start.2 = (bf16[32,32,1024]{2,1,0:T(8,128)(2,1)}, bf16[32,32,1024]{2,1,0:T(8,128)(2,1)}, u32[]{:S(2)}, u32[]{:S(2)}) collective-permute-start(bf16[32,32,1024]{2,1,0:T(8,128)(2,1)} %collective-permute-done.1), channel_id=1, source_target_pairs={{0,1},{1,2},{2,3},{3,0},{4,5},{5,6},{6,7},{7,4},{8,9},{9,10},{10,1... | collective-permute-start | bytes 6291464 | tf_op jit(solution)/shard_map/ppermute | solution.py:13
  98.1 59.7 %all-to-all-start.1 = ((s32[64,1,1]{2,1,0:T(1,128)}), s32[64,1,1]{2,1,0:T(1,128)S(1)}, u32[]{:S(2)}, u32[]{:S(2)}) async-start(s32[64,1,1]{2,1,0:T(1,128)} %copy.52), calls=%async_computation.1 | async-start | bytes 65536 | tf_op jit(solution)/shard_map/all_to_all | solution.py:61
  114.1 31.5 %copy-start.4 = (bf16[32,32,1024]{2,1,0:T(8,128)(2,1)S(1)}, bf16[32,32,1024]{2,1,0:T(8,128)(2,1)}, u32[]{:S(2)}) copy-start(bf16[32,32,1024]{2,1,0:T(8,128)(2,1)} %copy-done.3) | copy-start | bytes 6291460
  148.5 9.3 %copy-start.6 = (s32[32]{0:T(128)S(1)}, s32[32]{0:T(128)}, u32[]{:S(2)}) copy-start(s32[32]{0:T(128)} %param.10) | copy-start | bytes 388
  158.4 54.4 %all-to-all-start = ((s32[64,1,32]{2,1,0:T(1,128)}), s32[64,1,32]{2,1,0:T(1,128)S(1)}, u32[]{:S(2)}, u32[]{:S(2)}) async-start(s32[64,1,32]{2,1,0:T(1,128)} %broadcast_in_dim.42), calls=%async_computation | async-start | bytes 65536 | tf_op jit(solution)/shard_map/all_to_all | solution.py:62
  212.9 12.0 %copy-start.7 = (s32[8,2]{0,1:T(2,128)S(1)}, s32[8,2]{0,1:T(2,128)}, u32[]{:S(2)}) copy-start(s32[8,2]{0,1:T(2,128)} %param.13) | copy-start | bytes 196
  212.9 376.3 %all-to-all-start.3 = ((bf16[64,1,128,1024]{3,2,1,0:T(8,128)(2,1)}), bf16[64,1,128,1024]{3,2,1,0:T(8,128)(2,1)}, u32[]{:S(2)}, u32[]{:S(2)}) async-start(bf16[64,1,128,1024]{3,2,1,0:T(8,128)(2,1)} %bitcast.89), calls=%async_computation.3 | async-start | bytes 33554432 | tf_op jit(solution)/shard_map/all_to_all | solution.py:60
  589.2 125.3 %all-to-all-start.2 = ((s32[64,1,2]{2,1,0:T(1,128)}), s32[64,1,2]{2,1,0:T(1,128)S(1)}, u32[]{:S(2)}, u32[]{:S(2)}) async-start(s32[64,1,2]{2,1,0:T(1,128)} %copy.53), calls=%async_computation.2 | async-start | bytes 65536 | tf_op jit(solution)/shard_map/all_to_all | solution.py:104
  714.5 10.5 %copy-start.5 = (f32[4096]{0:T(1024)S(1)}, f32[4096]{0:T(1024)}, u32[]{:S(2)}) copy-start(f32[4096]{0:T(1024)} %param.15) | copy-start | bytes 49156
  714.5 196.2 %copy-start.8 = (f32[128]{0:T(128)S(1)}, f32[128]{0:T(128)}, u32[]{:S(2)}) copy-start(f32[128]{0:T(128)} %param.14) | copy-start | bytes 1540
  714.5 196.2 %all-to-all-start.4 = ((bf16[64,1,128,2,256]{4,3,2,1,0:T(2,128)(2,1)}), bf16[64,1,128,2,256]{4,3,2,1,0:T(2,128)(2,1)}, u32[]{:S(2)}, u32[]{:S(2)}) async-start(bf16[64,1,128,2,256]{4,3,2,1,0:T(2,128)(2,1)} %bitcast.91), calls=%async_computation.4 | async-start | bytes 16777216 | tf_op jit(solution)/shard_map/all_to_all | solution.py:97
  910.7 15.4 %copy-start.1 = (s32[16384]{0:T(1024)S(1)}, s32[16384]{0:T(1024)}, u32[]{:S(2)}) copy-start(s32[16384]{0:T(1024)} %param.11) | copy-start | bytes 196612
